TPU v7x, 32 devices: a whole 2x2x4 slice. The times are simulated.
32 devices in a mesh: dp: 4 (over y, x), mp: 8 (over z, core).
Axes of the slice: x: 2, y: 2, z: 4, core: 2. Of those that a mesh axis runs over, the one named last changes fastest.
Arguments:
- features: bfloat16 [1536, 8192], P('dp', 'mp'), may hold values from -6 to 6
- cotangent: bfloat16 [1536, 8192], P('dp', 'mp'), may hold values from -6 to 6
- weights: bfloat16 [2, 8192, 8192], P(None, 'mp'), may hold values from -0.0625 to 0.0625
- biases: float32 [2, 8192], P(None, 'mp'), may hold values from -3 to 3
- weight_accum: float32 [2, 8192], P(None, ('mp', 'dp')), may hold values from 100 to 16000
- owner_slot: int32 [128], replicated, may hold values from 0 to 127, each once
- bag_ids: int32 [128, 1536, 4], P(('dp', 'mp')), may hold values from 0 to 8191
- bag_length: int32 [128, 1536], P(('dp', 'mp')), may hold values from 1 to 4, as said below
- tables: float32 [128, 8192, 64], P(('dp', 'mp')), may hold values from -3 to 3
- table_accum: float32 [128, 8192], P(('dp', 'mp')), may hold values from 1 to 256
Outputs:
- weight_step: float32 [2, 8192, 8192], P(None, ('mp', 'dp'))
- new_weight_accum: float32 [2, 8192], P(None, ('mp', 'dp'))
- new_tables: float32 [128, 8192, 64], P(('dp', 'mp'))
- new_table_accum: float32 [128, 8192], P(('dp', 'mp'))
Inputs may be any that keep to these rules, and one draw needn't show every extreme that they name: `owner_slot`: A permutation; the owner slot s lies on device s // 4 in the order of dp+mp, as its entry s % 4. Only the first bag_length ids of a bag are looked up.
All inputs are finite; a program needn't handle non-finite values.
Results may differ from a plain program's by a relative error of at most 0.025.
Values may be sent and summed in bfloat16 or wider, within the bound.
No kernel may reach another device: no remote copies, remote signals or barrier semaphores. Data moves between devices by JAX's collectives and lax.ppermute only.
A program may use at most 192 MiB of HBM per device.

v0:
```python
import jax
import jax.numpy as jnp
from jax import lax
from jax.sharding import PartitionSpec as P

learn_rate = 0.5


def update_rows(grads, row_ids, length, table, accum):
    in_bag = jnp.arange(row_ids.shape[1], dtype=jnp.int32)[None, :] < length[:, None]
    spread = jnp.where(in_bag[:, :, None], grads.astype(jnp.float32)[:, None, :], jnp.float32(0.0))
    summed = jax.ops.segment_sum(
        spread.reshape(-1, grads.shape[1]), row_ids.reshape(-1), num_segments=table.shape[0]
    )
    renewed = accum + jnp.mean(summed * summed, axis=1)
    return (table - learn_rate * summed / jnp.sqrt(renewed)[:, None], renewed)


def deliver(slotted):
    count, tables_all, embed = slotted.shape
    data_size = lax.axis_size("dp")
    model_size = lax.axis_size("mp")
    per_device = tables_all // (data_size * model_size)
    direct = slotted.reshape(1, count, data_size * model_size, per_device, embed)
    arrived = lax.all_to_all(direct, ("dp", "mp"), split_axis=2, concat_axis=0, tiled=True)
    return arrived.reshape(data_size, model_size, count, per_device, embed)


def body(
    features,
    cotangent,
    weights,
    biases,
    weight_accum,
    owner_slot,
    bag_ids,
    bag_length,
    tables,
    table_accum,
):
    depth = weights.shape[0]
    block_cols = weights.shape[1]
    full_width = weights.shape[2]
    model_index = lax.axis_index("mp")
    base_f32 = features.astype(jnp.float32)
    current = features
    layer_inputs = []
    preacts = []
    for layer_idx in range(depth):
        gathered = lax.all_gather(current, "mp", axis=1, tiled=True)
        preact = (
            lax.dot_general(
                gathered,
                weights[layer_idx],
                (((1,), (1,)), ((), ())),
                preferred_element_type=jnp.float32,
            )
            + biases[layer_idx]
        )
        layer_inputs.append(gathered)
        preacts.append(preact)
        if layer_idx + 1 < depth:
            current = (base_f32 * preact + current.astype(jnp.float32)).astype(jnp.bfloat16)
    upstream = cotangent.astype(jnp.float32)
    carried = jnp.zeros_like(upstream)
    updates = [None] * depth
    accums = [None] * depth
    share = block_cols // lax.axis_size("dp")
    partial_value = None
    for layer_idx in range(depth - 1, -1, -1):
        scaled = (upstream * base_f32).astype(jnp.bfloat16)
        carried = carried + upstream * preacts[layer_idx]
        gathered = layer_inputs[layer_idx]

        def weight_term(start, count, scaled=scaled, gathered=gathered):
            return lax.dot_general(
                scaled, gathered, (((0,), (0,)), ((), ())), preferred_element_type=jnp.float32
            )

        weight_grad = lax.psum_scatter(
            weight_term(jnp.int32(0), share * lax.axis_size("dp")).astype(jnp.bfloat16),
            "dp",
            scatter_dimension=0,
            tiled=True,
        ).astype(jnp.float32)
        renewed = weight_accum[layer_idx] + jnp.mean(weight_grad * weight_grad, axis=1)
        updates[layer_idx] = weight_grad / jnp.sqrt(renewed)[:, None]
        accums[layer_idx] = renewed
        partial_value = jnp.dot(scaled, weights[layer_idx], preferred_element_type=jnp.float32)
        if layer_idx > 0:
            upstream = upstream + lax.psum_scatter(
                partial_value.astype(jnp.bfloat16), "mp", scatter_dimension=1, tiled=True
            ).astype(jnp.float32)
    start_col = model_index * block_cols
    own_cols = (
        lax.dynamic_slice_in_dim(partial_value, start_col, block_cols, 1) + upstream + carried
    )
    partial_value = lax.dynamic_update_slice_in_dim(partial_value, own_cols, start_col, 1)
    tables_all = owner_slot.shape[0]
    embed = full_width // tables_all
    inverse = (
        jnp.zeros((tables_all,), jnp.int32)
        .at[owner_slot]
        .set(jnp.arange(tables_all, dtype=jnp.int32))
    )
    my_rows = lax.psum_scatter(
        partial_value.astype(jnp.bfloat16), "mp", scatter_dimension=0, tiled=True
    )
    slotted = jnp.take(my_rows.reshape(my_rows.shape[0], tables_all, embed), inverse, axis=1)
    arrived = deliver(slotted)
    pooled = arrived.reshape(-1, arrived.shape[3], arrived.shape[4])
    new_tables, new_accum = jax.vmap(update_rows, in_axes=(1, 0, 0, 0, 0))(
        pooled, bag_ids, bag_length, tables, table_accum
    )
    return (jnp.stack(updates), jnp.stack(accums), new_tables, new_accum)


def solution(mesh):
    return jax.shard_map(
        body,
        mesh=mesh,
        in_specs=(
            P("dp", "mp"),
            P("dp", "mp"),
            P(None, "mp", None),
            P(None, "mp"),
            P(None, ("mp", "dp")),
            P(),
            P(("dp", "mp"), None, None),
            P(("dp", "mp"), None),
            P(("dp", "mp"), None, None),
            P(("dp", "mp"), None),
        ),
        out_specs=(
            P(None, ("mp", "dp"), None),
            P(None, ("mp", "dp")),
            P(("dp", "mp"), None, None),
            P(("dp", "mp"), None),
        ),
        check_vma=False,
    )
```

profile of v0, /device:TPU:0, one launch (start us, length us, event | category | flops | bytes accessed | tf_op | source)
XLA Modules:
  0.0 645.5 jit_solution(161048640601415832)
XLA Ops:
  7.2 0.0 all-gather.3.cloned.1.call-start
  7.2 0.7 all-gather.3.cloned.1.call-update
  7.9 0.0 reduce-scatter.5.cloned.1.call-start
  7.9 12.3 %fusion.12 = bf16[384,8192]{1,0:T(8,128)(2,1)} fusion(bf16[2,1024,8192]{2,1,0:T(8,128)(2,1)} %param.12, bf16[384,1024]{1,0:T(8,128)(2,1)} %param.10, bf16[384,1024]{1,0:T(8,128)(2,1)} %param.11), kind=kOutput, calls=%fused_computation.19 | convolution fusion | flops 6447169536 | bytes 24641536 | tf_op jit(solution)/shard_map/dot_general | solution.py:89
  20.2 0.0 reduce-scatter.5.cloned.1.call-update
  20.3 0.0 all-gather.5.cloned.1.call-start
  20.3 0.6 copy-done.7
  20.9 56.1 %all-gather.3.cloned.1.call-done = bf16[384,8192]{1,0:T(8,128)(2,1)} async-done(((bf16[384,1024]{1,0:T(8,128)(2,1)}), bf16[384,8192]{1,0:T(8,128)(2,1)}) %all-gather.3.cloned.1.call-update) | async-done | bytes 6291472 | tf_op jit(solution)/shard_map/all_gather | solution.py:50
  77.0 13.3 %fusion.26 = (bf16[384,1024]{1,0:T(8,128)(2,1)}, f32[384,1024]{1,0:T(8,128)}) fusion(bf16[384,1024]{1,0:T(8,128)(2,1)S(1)} %copy-done.1, f32[1024]{0:T(1024)S(1)} %bitcast.63, bf16[384,8192]{1,0:T(8,128)(2,1)} %all-gather.3.cloned.1.call-done, bf16[2,1024,8192]{2,1,0:T(8,128)(2,1)} %param.12), kind=kOutput, calls=%fused_computation.45 | convolution fusion | flops 6444417024 | bytes 26218496 | tf_op jit(solution)/shard_map/dot_general | solution.py:52
  90.3 0.0 all-gather.5.cloned.1.call-update
  90.3 0.6 reduce-scatter.11.cloned.1.call-start
  90.9 57.4 %reduce-scatter.5.cloned.1.call-done = bf16[384,1024]{1,0:T(8,128)(2,1)} async-done(((bf16[384,8192]{1,0:T(8,128)(2,1)}), bf16[384,1024]{1,0:T(8,128)(2,1)}) %reduce-scatter.5.cloned.1.call-update) | async-done | bytes 786448 | tf_op jit(solution)/shard_map/reduce_scatter | solution.py:91
  148.3 15.3 %fusion = f32[384,8192]{1,0:T(8,128)} fusion(bf16[2,1024,8192]{2,1,0:T(8,128)(2,1)} %param.12, bf16[384,1024]{1,0:T(8,128)(2,1)S(1)} %copy-done.1, bf16[384,1024]{1,0:T(8,128)(2,1)} %reduce-scatter.5.cloned.1.call-done, bf16[384,1024]{1,0:T(8,128)(2,1)S(1)} %copy-done.2), kind=kOutput, calls=%fused_computation.4 | convolution fusion | flops 6444810240 | bytes 31719424 | tf_op jit(solution)/shard_map/dot_general | solution.py:89
  163.6 49.5 %all-gather.5.cloned.1.call-done = bf16[384,8192]{1,0:T(8,128)(2,1)} async-done(((bf16[384,1024]{1,0:T(8,128)(2,1)}), bf16[384,8192]{1,0:T(8,128)(2,1)}) %all-gather.5.cloned.1.call-update) | async-done | bytes 6291472 | tf_op jit(solution)/shard_map/all_gather | solution.py:50
  213.1 13.9 %fusion.23 = f32[384,8192]{1,0:T(8,128)} fusion(f32[384,8192]{1,0:T(8,128)} %fusion, s32[]{:T(128)S(6)} %select_n.30, bf16[384,1024]{1,0:T(8,128)(2,1)S(1)} %copy-done.2, bf16[384,1024]{1,0:T(8,128)(2,1)S(1)} %copy-done.3, f32[384,1024]{1,0:T(8,128)} %get-tuple-element.29, bf16[384,8192]{1,0:T(8,128)(2,1)} %all-gather.5.cloned.1.call-done, ...), kind=kOutput, calls=%fused_computation.42 | convolution fusion | flops 6446383104 | bytes 29368324 | tf_op jit(solution)/shard_map/dot_general | solution.py:52
  227.0 8.2 %convert_element_type.58 = bf16[384,8192]{1,0:T(8,128)(2,1)} convert(f32[384,8192]{1,0:T(8,128)} %fusion.23) | non-fusion elementwise | flops 3145728 | bytes 18874368 | tf_op jit(solution)/shard_map/convert_element_type | solution.py:107
  235.2 0.0 reduce-scatter.11.cloned.1.call-update
  235.2 0.0 reduce-scatter.7.cloned.1.call-start
  235.3 15.5 %convolution_convert_fusion.1 = bf16[1024,8192]{1,0:T(8,128)(2,1)} fusion(bf16[384,8192]{1,0:T(8,128)(2,1)} %all-gather.3.cloned.1.call-done, bf16[384,1024]{1,0:T(8,128)(2,1)S(1)} %copy-done.1, bf16[384,1024]{1,0:T(8,128)(2,1)S(1)} %copy-done.3, bf16[384,1024]{1,0:T(8,128)(2,1)S(1)} %copy-done.2), kind=kOutput, calls=%fused_computation.14 | convolution fusion | flops 6453198848 | bytes 25427968 | tf_op jit(solution)/shard_map/dot_general | solution.py:76
  250.8 0.0 reduce-scatter.7.cloned.1.call-update
  250.8 0.2 reduce-scatter.9.cloned.1.call-start
  251.0 15.3 %convolution_convert_fusion = bf16[1024,8192]{1,0:T(8,128)(2,1)} fusion(bf16[384,8192]{1,0:T(8,128)(2,1)} %all-gather.5.cloned.1.call-done, bf16[384,1024]{1,0:T(8,128)(2,1)S(1)} %copy-done.1, bf16[384,1024]{1,0:T(8,128)(2,1)S(1)} %copy-done.2), kind=kOutput, calls=%fused_computation.13 | convolution fusion | flops 6452412416 | bytes 24641536 | tf_op jit(solution)/shard_map/dot_general | solution.py:76
  266.3 0.0 reduce-scatter.9.cloned.1.call-update
  266.4 0.6 copy-done.11
  267.0 1.0 scatter_custom_fusion
  268.0 0.1 broadcast_in_dim.52
  268.1 0.1 lt.36
  268.2 0.4 lt.37
  268.6 1.1 copy.37
  269.7 2.7 reshape.84
  272.4 0.1 multiply_reduce_fusion.1
  272.5 0.2 and_reduce_fusion
  272.7 31.1 %reduce-scatter.11.cloned.1.call-done = bf16[48,8192]{1,0:T(8,128)(2,1)} async-done(((bf16[384,8192]{1,0:T(8,128)(2,1)}), bf16[48,8192]{1,0:T(8,128)(2,1)}) %reduce-scatter.11.cloned.1.call-update) | async-done | bytes 786448 | tf_op jit(solution)/shard_map/reduce_scatter | solution.py:106
  303.8 2.5 reshape.85
  306.3 0.0 copy-start.6
  306.3 2.2 copy.38
  308.5 2.3 gather_fusion
  310.7 0.2 fusion.37
  311.0 1.9 reshape.126
  312.8 3.6 all-to-all-start
  316.5 0.9 lt.39
  317.3 2.7 lt.40
  320.1 18.2 %all-to-all-done = bf16[32,2,6144]{2,1,0:T(2,128)(2,1)} async-done(((bf16[32,2,6144]{2,1,0:T(2,128)(2,1)}), bf16[32,2,6144]{2,1,0:T(2,128)(2,1)}, u32[]{:S(2)}, u32[]{:S(2)}) %all-to-all-start) | async-done | bytes 786464 | tf_op jit(solution)/shard_map/all_to_all | solution.py:25
  338.2 3.8 reshape.127
  342.0 1.8 convert_bitcast_fusion
  343.8 4.5 copy.40
  348.3 5.4 reshape.96
  353.7 2.1 copy.41
  355.8 2.3 broadcast_in_dim.56
  358.1 5.5 broadcast_select_fusion
  363.6 138.4 %scatter_custom_fusion.1 = f32[32768,64]{1,0:T(8,128)} fusion(s32[24576]{0:T(1024)S(1)} %bitcast.61, f32[24576,64]{1,0:T(8,128)} %bitcast.58, f32[]{:T(128)} %constant.11.clone.1), kind=kCustom, calls=%fused_computation.29 | custom fusion | flops 1572864 | bytes 8389120
  502.0 12.9 %copy.42 = f32[32768,64]{0,1:T(8,128)} copy(f32[32768,64]{1,0:T(8,128)} %scatter_custom_fusion.1) | data formatting | bytes 16777216
  515.0 7.6 %broadcast_multiply_fusion = f32[32768,64]{0,1:T(8,128)} fusion(f32[32768,64]{0,1:T(8,128)} %copy.42), kind=kLoop, calls=%fused_computation.32 | loop fusion | flops 2097152 | bytes 16777216 | tf_op jit(solution)/shard_map/vmap()/mul | solution.py:16
  522.6 11.6 %reshape.91 = f32[4,8192,64]{1,0,2:T(4,128)} reshape(f32[32768,64]{0,1:T(8,128)} %broadcast_multiply_fusion) | data formatting | bytes 16777216 | tf_op jit(solution)/shard_map/vmap()/mul | solution.py:16
  534.2 8.7 %multiply_reduce_fusion = f32[32768]{0:T(1024)S(1)} fusion(f32[32768,64]{1,0:T(8,128)} %scatter_custom_fusion.1), kind=kLoop, calls=%fused_computation.12 | loop fusion | flops 4161536 | bytes 8519680 | tf_op jit(solution)/shard_map/vmap()/reduce_sum | solution.py:15
  543.0 0.7 fusion.35
  543.7 11.5 %divide_subtract_fusion = f32[4,8192,64]{1,0,2:T(4,128)S(1)} fusion(f32[4,8192,64]{1,0,2:T(4,128)} %reshape.91, f32[4,8192,64]{1,2,0:T(8,128)} %param.18, f32[4,8192]{1,0:T(4,128)S(1)} %get-tuple-element.20), kind=kLoop, calls=%fused_computation.24 | loop fusion | flops 4194304 | bytes 25296896 | tf_op jit(solution)/shard_map/vmap()/sub | solution.py:16
  555.2 8.3 %copy.44 = f32[4,8192,64]{1,2,0:T(8,128)} copy(f32[4,8192,64]{1,0,2:T(4,128)S(1)} %divide_subtract_fusion) | data formatting | bytes 16777216
  563.4 3.1 fusion.15
  566.6 58.0 %reduce-scatter.9.cloned.1.call-done = bf16[256,8192]{1,0:T(8,128)(2,1)} async-done(((bf16[1024,8192]{1,0:T(8,128)(2,1)}), bf16[256,8192]{1,0:T(8,128)(2,1)}) %reduce-scatter.9.cloned.1.call-update) | async-done | bytes 4194320 | tf_op jit(solution)/shard_map/reduce_scatter | solution.py:80
  624.6 3.3 fusion.17
  627.9 0.6 pad_maximum_fusion.1
  628.5 3.7 fusion.16
  632.2 6.2 pad_maximum_fusion
  (39 shorter events, 0.3 us)
Async XLA Ops:
  7.2 69.9 %all-gather.3.cloned.1.call-start = ((), (), s32[]{:S(2)}) async-start(), calls=%async_computation.6 | async-start | bytes 7077888 | tf_op jit(solution)/shard_map/all_gather | solution.py:50
  7.9 140.4 %reduce-scatter.5.cloned.1.call-start = ((), (), s32[]{:S(2)}) async-start(), calls=%async_computation.5 | async-start | bytes 7077888 | tf_op jit(solution)/shard_map/reduce_scatter | solution.py:91
  20.2 0.7 copy-start.7
  20.2 56.8 %copy-start.1 = (bf16[384,1024]{1,0:T(8,128)(2,1)S(1)}, bf16[384,1024]{1,0:T(8,128)(2,1)}, u32[]{:S(2)}) copy-start(bf16[384,1024]{1,0:T(8,128)(2,1)} %param.10) | copy-start | bytes 2359300
  20.3 192.9 %all-gather.5.cloned.1.call-start = ((), (), s32[]{:S(2)}) async-start(), calls=%async_computation.8 | async-start | bytes 7077888 | tf_op jit(solution)/shard_map/all_gather | solution.py:50
  77.0 71.3 %copy-start.2 = (bf16[384,1024]{1,0:T(8,128)(2,1)S(1)}, bf16[384,1024]{1,0:T(8,128)(2,1)}, u32[]{:S(2)}) copy-start(bf16[384,1024]{1,0:T(8,128)(2,1)} %param.11) | copy-start | bytes 2359300
  90.3 213.5 %reduce-scatter.11.cloned.1.call-start = ((), (), s32[]{:S(2)}) async-start(), calls=%async_computation.10 | async-start | bytes 7077888 | tf_op jit(solution)/shard_map/reduce_scatter | solution.py:106
  148.3 64.8 %copy-start.3 = (bf16[384,1024]{1,0:T(8,128)(2,1)S(1)}, bf16[384,1024]{1,0:T(8,128)(2,1)}, u32[]{:S(2)}) copy-start(bf16[384,1024]{1,0:T(8,128)(2,1)} %reduce-scatter.5.cloned.1.call-done) | copy-start | bytes 2359300
  235.2 328.2 %reduce-scatter.7.cloned.1.call-start = ((), (), s32[]{:S(2)}) async-start(), calls=%async_computation.7 | async-start | bytes 20971520 | tf_op jit(solution)/shard_map/reduce_scatter | solution.py:80
  250.8 373.8 %reduce-scatter.9.cloned.1.call-start = ((), (), s32[]{:S(2)}) async-start(), calls=%async_computation.9 | async-start | bytes 20971520 | tf_op jit(solution)/shard_map/reduce_scatter | solution.py:80
  266.3 0.7 copy-start.11
  266.3 2.3 copy-start.5
  267.0 5.4 copy-start.10
  267.0 5.5 copy-start.9
  306.3 10.2 %copy-start.6 = (s32[4,1536]{1,0:T(4,128)S(1)}, s32[4,1536]{1,0:T(4,128)}, u32[]{:S(2)}) copy-start(s32[4,1536]{1,0:T(4,128)} %param.17) | copy-start | bytes 73732
  312.8 25.4 %all-to-all-start = ((bf16[32,2,6144]{2,1,0:T(2,128)(2,1)}), bf16[32,2,6144]{2,1,0:T(2,128)(2,1)}, u32[]{:S(2)}, u32[]{:S(2)}) async-start(bf16[32,2,6144]{2,1,0:T(2,128)(2,1)} %reshape.126), calls=%async_computation.4 | async-start | bytes 1572864 | tf_op jit(solution)/shard_map/all_to_all | solution.py:25
  534.2 8.8 %copy-start.4 = (f32[4,8192]{1,0:T(4,128)S(1)}, f32[4,8192]{1,0:T(4,128)}, u32[]{:S(2)}) copy-start(f32[4,8192]{1,0:T(4,128)} %param.19) | copy-start | bytes 393220
  563.4 64.4 %copy-start.8 = (f32[2,256]{1,0:T(2,128)S(1)}, f32[2,256]{1,0:T(2,128)}, u32[]{:S(2)}) copy-start(f32[2,256]{1,0:T(2,128)} %param.14) | copy-start | bytes 6148
  624.6 3.9 copy-start
Sparse Core Ops, SparseCore 0:
  9.6 67.4 all-gather.2
  79.9 68.3 reduce-scatter.4
  149.9 63.1 all-gather.4
  235.4 68.3 reduce-scatter.10
  307.3 160.5 reduce-scatter.6
  470.8 153.7 reduce-scatter.8
where the time goes:
time: 651 us; the launch traced here: 645 us
  waiting for transfers between devices  271 us (42%)
  other arithmetic  200 us (31%)
  matrix products  85.6 us (13%)
  local copies, waits for them, and re-layouts  69.9 us (11%)
  between operations  14.6 us (2%)
    unnamed x5, other arithmetic  139 us
    all_gather x2, waiting for transfers between devices, body(): gathered = lax.all_gather(current, 'mp', axis=1, tiled=True)  106 us
    reduce_scatter x2, waiting for transfers between devices, body(): lax.psum_scatter(partial_value.astype(jnp.bfloat16), 'mp', scatter_dimens...  88.5 us
    reduce_scatter x2, waiting for transfers between devices, body(): lax.psum_scatter(weight_term(jnp.int32(0), share * lax.axis_size('dp')).a...  58 us
    dot_general x2, matrix products, weight_term(): lax.dot_general(scaled, gathered, (((0,), (0,)), ((), ())), preferred_ele...  30.8 us
    unnamed x31, local copies, waits for them, and re-layouts  29.2 us
    dot_general x2, matrix products, body(): jnp.dot(scaled, weights[layer_idx], preferred_element_type=jnp.float32)  27.6 us
    dot_general x2, matrix products, body(): lax.dot_general(gathered, weights[layer_idx], (((1,), (1,)), ((), ())), p...  27.2 us
  transfers between devices with their start and end apart: 7, of which 6 were waited for; matrix products, arithmetic and copies ran while one was open for 49% of the time, Pallas kernels for 0%

commit v1 on v0

v1 whole, which is shorter than its diff:
```python
import functools
import jax, jax.numpy as jnp
from jax import lax
from jax.experimental import pallas as pl
from jax.experimental.pallas import tpu as pltpu
from jax.sharding import PartitionSpec as P


learn_rate = 0.5
cores = 2


def embed_kernel(n_tab, bag, batch, embed, chunk, unroll, rate, ids_ref, g_ref, tab_ref, acc_in_ref, tab_out, acc_out, rows, *accs):
    step = pl.program_id(0)
    pairs = g_ref.shape[1]

    @pl.when(step == 0)
    def _():
        src, _, per, lanes = g_ref.shape
        for a in accs:
            a[...] = jnp.zeros_like(a)
        for p in range(pairs):
            rows[p] = g_ref[:, p].astype(jnp.float32).reshape(src * per, lanes)

        def one(i, carry):
            for u in range(unroll):
                b = i * unroll + u
                vals = [rows[p, pl.ds(b, 1), :] for p in range(pairs)]
                for j in range(bag):
                    for t in range(n_tab):
                        v = ids_ref[(t * bag + j) * batch + b]
                        accs[t][pl.ds(v, 1), :] += vals[t // 2]
            return carry

        lax.fori_loop(0, batch // unroll, one, 0)

    base = pl.multiple_of(step * chunk, chunk)
    for p in range(pairs):
        first = accs[2 * p][pl.ds(base, chunk), :]
        if 2 * p + 1 < n_tab:
            second = accs[2 * p + 1][pl.ds(base, chunk), :]
            lane = lax.broadcasted_iota(jnp.int32, first.shape, 1)
            first = jnp.where(lane < embed, first, second)
        turned = first.T
        for o in range(min(2, n_tab - 2 * p)):
            t = 2 * p + o
            grad = turned[o * embed:(o + 1) * embed, :]
            renewed = acc_in_ref[t:t + 1, :] + jnp.sum(grad * grad, axis=0, keepdims=True) * (1.0 / embed)
            acc_out[t:t + 1, :] = renewed
            tab_out[t] = tab_ref[t] - (rate * grad) / jnp.sqrt(renewed)


def embed_update(ids, grads, tables_t, accum, bag, batch, rate, chunk=1024, unroll=8):
    n_tab, embed, vocab = tables_t.shape
    chunk = min(chunk, vocab)
    kern = functools.partial(embed_kernel, n_tab, bag, batch, embed, chunk, unroll, rate)
    return pl.pallas_call(
        kern,
        out_shape=(jax.ShapeDtypeStruct(tables_t.shape, jnp.float32), jax.ShapeDtypeStruct(accum.shape, jnp.float32)),
        grid_spec=pltpu.PrefetchScalarGridSpec(
            num_scalar_prefetch=1,
            grid=(vocab // chunk,),
            in_specs=[
                pl.BlockSpec(grads.shape, lambda i, s: (0,) * 4, pipeline_mode=pl.Buffered(1)),
                pl.BlockSpec((n_tab, embed, chunk), lambda i, s: (0, 0, i)),
                pl.BlockSpec((n_tab, chunk), lambda i, s: (0, i)),
            ],
            out_specs=[
                pl.BlockSpec((n_tab, embed, chunk), lambda i, s: (0, 0, i)),
                pl.BlockSpec((n_tab, chunk), lambda i, s: (0, i)),
            ],
            scratch_shapes=[pltpu.VMEM((grads.shape[1], batch, grads.shape[3]), jnp.float32)]
            + [pltpu.VMEM((vocab + 8, grads.shape[3]), jnp.float32) for _ in range(n_tab)],
        ),
        compiler_params=pltpu.CompilerParams(dimension_semantics=("arbitrary",), vmem_limit_bytes=56 * 1024 * 1024),
        cost_estimate=pl.CostEstimate(flops=100000000, bytes_accessed=150000000, transcendentals=0),
        name="embed_update",
    )(ids, grads, tables_t, accum)


def tile_of(size, limit):
    return max(t for t in range(128, limit + 1, 128) if size % t == 0)


def turn_kernel(parts, index_ref, value_ref, turned_ref, own_ref, other_ref):
    share = own_ref.shape[1]
    width = value_ref.shape[1]
    for first in range(0, width, 128):
        turned_ref[first : first + 128, :] = value_ref[:, first : first + 128].T
    for which, out in enumerate((own_ref, other_ref)):
        for k in range(parts):
            start = pl.multiple_of(index_ref[which * parts + k] * share, share)
            out[k] = turned_ref[pl.ds(start, share), :]


def turn(sent_index, value, parts, share):
    rows, width = value.shape
    return pl.pallas_call(
        functools.partial(turn_kernel, parts),
        out_shape=[
            jax.ShapeDtypeStruct((width, rows), value.dtype),
            jax.ShapeDtypeStruct((parts, share, rows), value.dtype),
            jax.ShapeDtypeStruct((parts, share, rows), value.dtype),
        ],
        grid_spec=pltpu.PrefetchScalarGridSpec(
            num_scalar_prefetch=1,
            grid=(1,),
            in_specs=[pl.BlockSpec((rows, width), lambda i, s: (0, 0))],
            out_specs=[
                pl.BlockSpec((width, rows), lambda i, s: (0, 0)),
                pl.BlockSpec((parts, share, rows), lambda i, s: (0, 0, 0)),
                pl.BlockSpec((parts, share, rows), lambda i, s: (0, 0, 0)),
            ],
        ),
        compiler_params=pltpu.CompilerParams(vmem_limit_bytes=16 * 1024 * 1024),
        cost_estimate=pl.CostEstimate(
            flops=rows * width, bytes_accessed=8 * rows * width, transcendentals=0
        ),
        name="turn",
    )(sent_index, value)


def grad_kernel(parts, index_ref, *refs):
    mine, near = refs[:parts], refs[parts]
    own, nxt = refs[parts + 1][...], refs[parts + 2][...]
    outs = refs[parts + 3 :]
    for k in range(parts):
        total = jnp.dot(mine[k][...], own, preferred_element_type=jnp.float32)
        total = total + jnp.dot(near[k], nxt, preferred_element_type=jnp.float32)
        outs[k][...] = total.astype(outs[k].dtype)


def half_grad(index, turned, near, wide, next_half):
    parts, share, rows = near.shape
    half = next_half.shape[1]
    tile = tile_of(half, 512)
    per_half = half // tile

    def chosen(k):
        return pl.BlockSpec((share, rows), lambda i, s: (s[1 + k], 0))

    return pl.pallas_call(
        functools.partial(grad_kernel, parts),
        out_shape=[jax.ShapeDtypeStruct((share, half), jnp.bfloat16) for _ in range(parts)],
        grid_spec=pltpu.PrefetchScalarGridSpec(
            num_scalar_prefetch=1,
            grid=(per_half,),
            in_specs=[chosen(k) for k in range(parts)]
            + [
                pl.BlockSpec(near.shape, lambda i, s: (0, 0, 0)),
                pl.BlockSpec((rows, tile), lambda i, s: (0, s[0] * per_half + i)),
                pl.BlockSpec((rows, tile), lambda i, s: (0, i)),
            ],
            out_specs=[pl.BlockSpec((share, tile), lambda i, s: (0, i)) for _ in range(parts)],
        ),
        compiler_params=pltpu.CompilerParams(vmem_limit_bytes=32 * 1024 * 1024),
        cost_estimate=pl.CostEstimate(
            flops=4 * parts * share * rows * half,
            bytes_accessed=4 * rows * half + 2 * parts * share * half,
            transcendentals=0,
        ),
        name="half_grad",
    )(index, *([turned] * parts), near, wide, next_half)


def blank(shape):
    return pl.pallas_call(
        lambda out_ref: None,
        out_shape=jax.ShapeDtypeStruct(shape, jnp.bfloat16),
        out_specs=pl.BlockSpec(memory_space=pl.ANY),
    )()


def after(value, *needed):
    return lax.optimization_barrier((value, *needed))[0]


def step_kernel(parts, side_ref, accum_ref, *refs):
    pieces, out_ref, new_ref = refs[: 2 * parts], refs[-2], refs[-1]
    width = out_ref.shape[2]
    half = width // 2
    sums = []
    for h in range(2):
        total = pieces[h * parts][...].astype(jnp.float32)
        for k in range(1, parts):
            total = total + pieces[h * parts + k][...].astype(jnp.float32)
        sums.append(total)
    square = jnp.sum(sums[0] * sums[0], axis=1, keepdims=True) + jnp.sum(
        sums[1] * sums[1], axis=1, keepdims=True
    )
    renewed = accum_ref[...] + square * (1.0 / width)
    new_ref[...] = renewed
    root = jnp.sqrt(renewed)
    side = side_ref[0]
    near = pl.multiple_of(side * half, 128)
    far = pl.multiple_of((1 - side) * half, 128)
    out_ref[0, :, pl.ds(near, half)] = sums[0] / root
    out_ref[0, :, pl.ds(far, half)] = sums[1] / root


def weight_update(side, accum, near_parts, far_parts, layer_idx, depth, whole):
    parts = len(near_parts)
    share, half = near_parts[0].shape
    tile = 32
    piece = pl.BlockSpec((tile, half), lambda i, s: (i, 0))
    single = pl.BlockSpec((tile, 1), lambda i, s: (i, 0))
    carried = [] if whole is None else [whole]
    return pl.pallas_call(
        functools.partial(step_kernel, parts),
        out_shape=[
            jax.ShapeDtypeStruct((depth, share, 2 * half), jnp.float32),
            jax.ShapeDtypeStruct((share, 1), jnp.float32),
        ],
        grid_spec=pltpu.PrefetchScalarGridSpec(
            num_scalar_prefetch=1,
            grid=(share // tile,),
            in_specs=[single] + [piece] * (2 * parts) + [pl.BlockSpec(memory_space=pl.ANY)] * len(carried),
            out_specs=[
                pl.BlockSpec((1, tile, 2 * half), lambda i, s: (layer_idx, i, 0)),
                single,
            ],
        ),
        input_output_aliases={2 + 2 * parts: 0} if carried else {},
        compiler_params=pltpu.CompilerParams(vmem_limit_bytes=32 * 1024 * 1024),
        cost_estimate=pl.CostEstimate(
            flops=8 * share * half,
            bytes_accessed=share * half * (8 + 4 * parts),
            transcendentals=0,
        ),
        name="weight_update",
    )(side, accum, *near_parts, *far_parts, *carried)


def slot_kernel(embed, per_device, table_ref, summed_ref, late_ref, out_ref, joined):
    width = late_ref.shape[2]
    for m in range(late_ref.shape[0]):
        cols = slice(m * width, (m + 1) * width)
        joined[:, cols] = summed_ref[:, cols] + late_ref[m].astype(jnp.float32)
    devices, pairs, rows, lanes = out_ref.shape
    lane = lax.broadcasted_iota(jnp.int32, (rows, lanes), 1)

    def look(slot):
        first = table_ref[slot] * embed
        start = pl.multiple_of(first // lanes * lanes, 128)
        value = joined[:, pl.ds(start, lanes)]
        return value, first - start

    def one(device, carry):
        for p in range(pairs):
            slot = device * per_device + 2 * p
            low, low_at = look(slot)
            high, high_at = look(slot + min(1, per_device - 1 - 2 * p))
            low = jnp.where(low_at == 0, low, pltpu.roll(low, embed, 1))
            high = jnp.where(high_at == 0, pltpu.roll(high, embed, 1), high)
            out_ref[device, p] = jnp.where(lane < embed, low, high).astype(out_ref.dtype)
        return carry

    lax.fori_loop(0, devices, one, 0)


def to_slots(table_of, summed, late, embed, devices):
    rows = summed.shape[0]
    per_device = table_of.shape[0] // devices
    pairs = (per_device + 1) // 2
    return pl.pallas_call(
        functools.partial(slot_kernel, embed, per_device),
        out_shape=jax.ShapeDtypeStruct((devices, pairs, rows, 2 * embed), jnp.bfloat16),
        grid_spec=pltpu.PrefetchScalarGridSpec(
            num_scalar_prefetch=1,
            grid=(1,),
            in_specs=[
                pl.BlockSpec(summed.shape, lambda i, s: (0, 0)),
                pl.BlockSpec(late.shape, lambda i, s: (0, 0, 0)),
            ],
            out_specs=pl.BlockSpec((devices, pairs, rows, 2 * embed), lambda i, s: (0, 0, 0, 0)),
            scratch_shapes=[pltpu.VMEM(summed.shape, jnp.float32)],
        ),
        compiler_params=pltpu.CompilerParams(vmem_limit_bytes=32 * 1024 * 1024),
        cost_estimate=pl.CostEstimate(
            flops=4 * rows * summed.shape[1],
            bytes_accessed=10 * rows * summed.shape[1],
            transcendentals=0,
        ),
        name="to_slots",
    )(table_of, summed, late)


def body(
    features,
    cotangent,
    weights,
    biases,
    weight_accum,
    owner_slot,
    bag_ids,
    bag_length,
    tables,
    table_accum,
):
    depth, block_cols, full_width = weights.shape
    data_size = lax.axis_size("dp")
    model_size = lax.axis_size("mp")
    line = model_size // cores
    model_index = lax.axis_index("mp")
    data_index = lax.axis_index("dp")
    spot = model_index // cores
    core = model_index % cores
    first_core = core == 0
    rows = features.shape[0]
    half = full_width // 2
    members = data_size // 2
    f32, bf16 = jnp.float32, jnp.bfloat16

    def swap(value):
        return lax.ppermute(value, "mp", [(i, i ^ 1) for i in range(model_size)])

    def hop(value, right, left):
        pairs = [(z * cores, (z + 1) * cores) for z in right]
        pairs += [(z * cores + 1, (z - 1) * cores + 1) for z in left]
        return lax.ppermute(value, "mp", pairs)

    def chip_pair(value):
        other = swap(value)
        return jnp.where(
            first_core,
            jnp.concatenate([value, other], axis=1),
            jnp.concatenate([other, value], axis=1),
        )

    def gather_and_reduce(chip, partial_value, axis, fill):
        width = chip.shape[1]
        size = partial_value.shape[axis] // line
        part = size // cores

        def block(at):
            return lax.dynamic_slice_in_dim(
                partial_value, jnp.clip(at, 0, line - 1) * size, size, axis
            )

        wide = lax.dynamic_update_slice_in_dim(blank((rows, full_width)), chip, spot * width, 1)
        moving = hop(chip, range(0, line - 1), range(1, line))
        moving = after(moving, partial_value)
        inbound = None
        for k in range(1, line):
            passed = swap(moving)
            ahead = None
            if k + 1 < line:
                ahead = hop(moving, range(k, line - 1), range(1, line - k))
            far = line - k
            away = jnp.where(first_core, far, -far)
            crossed = swap(block(spot - away))
            total = block(spot + away).astype(f32) + crossed.astype(f32)
            if inbound is not None:
                total = total + inbound.astype(f32)
            total = total.astype(bf16)
            inbound = hop(total, range(k), range(line - k, line))
            for piece, up in ((moving, first_core), (passed, ~first_core)):
                place = jnp.where(up, spot - k, spot + k)
                here = (place >= 0) & (place < line)
                wide = lax.dynamic_update_slice_in_dim(
                    wide, jnp.where(here, piece, chip), jnp.where(here, place, spot) * width, 1
                )
            if ahead is not None:
                moving = after(ahead, total, *fill(k, total))

        def finish(*needed):
            last = after(inbound, *needed)
            local = block(spot)

            def portion(at):
                return lax.dynamic_slice_in_dim(local, at * part, part, axis).astype(
                    f32
                ) + lax.dynamic_slice_in_dim(last, at * part, part, axis).astype(f32)

            return portion(core) + swap(portion(1 - core).astype(bf16)).astype(f32)

        return wide, finish

    def crossing(low_core, high_core):
        pairs = []
        for d in range(data_size):
            for m in range(model_size):
                target = (high_core if m % cores else low_core)(d)
                pairs.append((d * model_size + m, target * model_size + m))
        return pairs

    def cross(value, low_core, high_core):
        return lax.ppermute(value, ("dp", "mp"), crossing(low_core, high_core))

    low_flip = lambda d: d ^ 1
    top_flip = lambda d: (d + members) % data_size
    low_turn = lambda k: lambda d: (d // 2 + k) % members * 2 + d % 2
    top_turn = lambda k: lambda d: d // members * members + (d % members + k) % members
    low_bit, low_rest = data_index % 2, data_index // 2
    top_bit, top_rest = data_index // members, data_index % members

    side = core.astype(jnp.int32)
    share = block_cols // data_size
    own_low = (first_core, ~first_core)

    def row_blocks(which, flip):
        turns = jnp.arange(members, dtype=jnp.int32)
        low = (low_rest + turns) % members * 2 + (low_bit ^ flip)
        top = (top_bit ^ flip) * members + (top_rest + turns) % members
        return jnp.where(own_low[which], low, top).astype(jnp.int32)

    sent_index = jnp.concatenate([row_blocks(0, 1), row_blocks(1, 1)])
    grad_index = [
        jnp.concatenate([(side if which == 0 else 1 - side)[None], row_blocks(which, 0)])
        for which in range(2)
    ]
    flips = ((low_flip, top_flip), (top_flip, low_flip))

    def layer_neighbour(wide, *needed):
        start = after(core * half, *needed)
        sent = lax.dynamic_slice_in_dim(wide, start, half, 1)
        near = cross(sent, *flips[0])
        return (near, swap(near)), sent

    def turned_sums(scaled, *needed):
        turned, own_sent, other_sent = turn(after(sent_index, *needed), scaled, members, share)
        return turned, cross(own_sent, *flips[0]), cross(other_sent, *flips[1])

    def half_sums(turned, wide, neighbours, *needed):
        result = []
        for which in range(2):
            pieces = half_grad(
                after(grad_index[which], *needed),
                turned[0],
                turned[1 + which],
                wide,
                neighbours[which],
            )
            arrived = [pieces[0]]
            for k in range(1, members):
                turns = (low_turn(k), top_turn(k))
                arrived.append(cross(pieces[k], *(turns if which == 0 else turns[::-1])))
            result.append(arrived)
        return result

    base_f32 = features.astype(f32)
    top_up = cotangent.astype(f32)

    def preact_of(wide, layer_idx):
        product = lax.dot_general(
            wide, weights[layer_idx], (((1,), (1,)), ((), ())), preferred_element_type=f32
        )
        return product + biases[layer_idx]

    def partial_of(scaled, layer_idx):
        return jnp.dot(scaled, weights[layer_idx], preferred_element_type=f32).astype(bf16)

    chip = chip_pair(features)
    top_scaled = (after(cotangent, chip).astype(f32) * base_f32).astype(bf16)
    top_turned = []

    def fill_top(k, total):
        if k == 1:
            top_turned.extend(turned_sums(top_scaled, total))
            return (top_turned[0],)
        return ()

    first_wide, low_up = gather_and_reduce(chip, partial_of(top_scaled, 1), 1, fill_top)
    first_pre = preact_of(first_wide, 0)
    current = (base_f32 * first_pre + base_f32).astype(bf16)
    low_up = top_up + low_up(current)
    first_near, first_sent = layer_neighbour(first_wide, current)
    chip = chip_pair(current)
    low_scaled = (after(low_up, chip, first_sent) * base_f32).astype(bf16)
    low_turned, low_sums = [], []

    def fill_low(k, total):
        if k == 1:
            low_turned.extend(turned_sums(low_scaled, total))
            return (low_turned[0],)
        if k == 2:
            low_sums.extend(half_sums(low_turned, first_wide, first_near, total))
            return (low_sums[0][0], low_sums[1][0])
        return ()

    second_wide, summed = gather_and_reduce(chip, partial_of(low_scaled, 0), 0, fill_low)
    second_pre = preact_of(second_wide, 1)
    late = (low_up + low_up * first_pre + top_up * second_pre).astype(bf16)
    summed = summed(late)
    second_near, second_sent = layer_neighbour(second_wide, late)
    late = lax.all_to_all(
        late.reshape(model_size, rows // model_size, block_cols),
        "mp",
        split_axis=0,
        concat_axis=0,
        tiled=True,
    )
    tables_all = owner_slot.shape[0]
    embed = full_width // tables_all
    table_of = (
        jnp.zeros((tables_all,), jnp.int32)
        .at[owner_slot]
        .set(jnp.arange(tables_all, dtype=jnp.int32))
    )
    slotted = to_slots(after(table_of, second_sent), summed, late, embed, data_size * model_size)
    arrived = lax.all_to_all(slotted, ("dp", "mp"), split_axis=0, concat_axis=0, tiled=True)
    top_sums = half_sums(top_turned, second_wide, second_near, slotted)
    whole, low_accum = weight_update(
        after(side[None], slotted), weight_accum[0][:, None], *low_sums, 0, depth, None
    )
    arrived = after(arrived, top_sums[0][0], top_sums[1][0], low_accum)

    _, batch, bag = bag_ids.shape
    vocab = tables.shape[1]
    in_bag = jnp.arange(bag, dtype=jnp.int32)[None, None, :] < bag_length[:, :, None]
    ids = jnp.where(in_bag, bag_ids, vocab).transpose(0, 2, 1).reshape(-1)
    new_tables, new_accum = embed_update(
        ids, arrived, jnp.swapaxes(tables, 1, 2), table_accum, bag, batch, learn_rate
    )
    whole, top_accum = weight_update(
        after(side[None], new_accum), weight_accum[1][:, None], *top_sums, 1, depth, whole
    )
    accums = jnp.stack([low_accum[:, 0], top_accum[:, 0]])
    return (whole, accums, jnp.swapaxes(new_tables, 1, 2), new_accum)


def solution(mesh):
    return jax.shard_map(
        body,
        mesh=mesh,
        in_specs=(
            P("dp", "mp"),
            P("dp", "mp"),
            P(None, "mp", None),
            P(None, "mp"),
            P(None, ("mp", "dp")),
            P(),
            P(("dp", "mp"), None, None),
            P(("dp", "mp"), None),
            P(("dp", "mp"), None, None),
            P(("dp", "mp"), None),
        ),
        out_specs=(
            P(None, ("mp", "dp"), None),
            P(None, ("mp", "dp")),
            P(("dp", "mp"), None, None),
            P(("dp", "mp"), None),
        ),
        check_vma=False,
    )
```

time: 651 us -> 470 us (0.72)
  other arithmetic: 200 us -> 62.1 us
  waiting for transfers between devices: 271 us -> 141 us
  Pallas kernels: 0 us -> 109 us
  starting transfers between devices: 4.49 us -> 70.4 us
  local copies, waits for them, and re-layouts: 69.9 us -> 30 us
  matrix products: 85.6 us -> 46.6 us
  between operations: 14.6 us -> 1.42 us
    reduce_scatter x4 -> x0, waiting for transfers between devices: 146 us -> none  [the longest x2 88.5 us: body(): lax.psum_scatter(partial_value.astype(jnp.bfloat16), 'mp', scatter_dimens...]
    unnamed x5 -> x1, other arithmetic: 139 us -> 0.01 us
    pallas_call x0 -> x12, Pallas kernels: none -> 109 us  [the longest x1 48 us: embed_update(): pl.pallas_call(kern, out_shape=(jax.ShapeDtypeStruct(tables_t.shape, jnp....]
    all_gather x2 -> x0, waiting for transfers between devices: 106 us -> none  [body(): gathered = lax.all_gather(current, 'mp', axis=1, tiled=True)]
    ppermute x0 -> x40, waiting for transfers between devices: none -> 84.8 us  [the longest x12 45.1 us: hop(): return lax.ppermute(value, 'mp', pairs)]
    ppermute x0 -> x40, starting transfers between devices: none -> 64.1 us  [the longest x12 47.6 us: hop(): return lax.ppermute(value, 'mp', pairs)]
    dot_general x6 -> x4, matrix products: 85.6 us -> 46.6 us  [the longest x2 26.1 us: preact_of(): lax.dot_general(wide, weights[layer_idx], (((1,), (1,)), ((), ())), prefe...]
    all_to_all x1 -> x2, waiting for transfers between devices: 18.2 us -> 56.4 us  [the longest x1 39.8 us: body(): lax.all_to_all(slotted, ('dp', 'mp'), split_axis=0, concat_axis=0, tiled=...]
  transfers between devices with their start and end apart: 7 -> 42, of which waited for: 6 -> 11; matrix products, arithmetic and copies ran while one was open for 49% -> 27% of each run, Pallas kernels for 0% -> 22%
where the time goes in v1:
time: 470 us; the launch traced here: 461 us
  waiting for transfers between devices  141 us (30%)
  Pallas kernels  109 us (23%)
  starting transfers between devices  70.4 us (15%)
  other arithmetic  62.1 us (13%)
  matrix products  46.6 us (10%)
  local copies, waits for them, and re-layouts  30 us (6%)
    pallas_call x1, Pallas kernels, embed_update(): pl.pallas_call(kern, out_shape=(jax.ShapeDtypeStruct(tables_t.shape, jnp....  48 us
    ppermute x12, starting transfers between devices, hop(): return lax.ppermute(value, 'mp', pairs)  47.6 us
    ppermute x12, waiting for transfers between devices, hop(): return lax.ppermute(value, 'mp', pairs)  45.1 us
    all_to_all x1, waiting for transfers between devices, body(): lax.all_to_all(slotted, ('dp', 'mp'), split_axis=0, concat_axis=0, tiled=...  39.8 us
    ppermute x10, waiting for transfers between devices, cross(): return lax.ppermute(value, ('dp', 'mp'), crossing(low_core, high_core))  37.5 us
    pallas_call x4, Pallas kernels, half_grad(): pl.pallas_call(functools.partial(grad_kernel, parts), out_shape=[jax.Shap...  36.9 us
    dot_general x2, matrix products, preact_of(): lax.dot_general(wide, weights[layer_idx], (((1,), (1,)), ((), ())), prefe...  26.1 us
    dynamic_update_slice x12, other arithmetic, gather_and_reduce(): lax.dynamic_update_slice_in_dim(wide, jnp.where(here, piece, chip), jnp.w...  23.1 us
  transfers between devices with their start and end apart: 42, of which 11 were waited for; matrix products, arithmetic and copies ran while one was open for 27% of the time, Pallas kernels for 22%

profile of v1, /device:TPU:0, one launch (start us, length us, event | category | flops | bytes accessed | tf_op | source)
XLA Modules:
  0.0 460.8 jit_solution(9751045107070697403)
XLA Ops:
  1.2 2.1 collective-permute-done
  3.3 1.9 constant_dynamic-update-slice_fusion.1
  5.2 6.0 %collective-permute-start.1 = (bf16[384,2048]{1,0:T(8,128)(2,1)S(1)}, bf16[384,2048]{1,0:T(8,128)(2,1)}, u32[]{:S(2)}, u32[]{:S(2)}) collective-permute-start(bf16[384,2048]{1,0:T(8,128)(2,1)S(1)} %get-tuple-element.91), channel_id=1, source_target_pairs={{0,2},{2,4},{4,6},{3,1},{5,3},{7,5},{8,10},{10,12},{12,14},{11,9},... | collective-permute-start | bytes 4718600 | tf_op jit(solution)/shard_map/ppermute | solution.py:320
  11.5 10.3 %fusion.12 = bf16[384,8192]{1,0:T(8,128)(2,1)S(1)} fusion(bf16[384,1024]{1,0:T(8,128)(2,1)S(1)} %fusion.20.value_ref, bf16[2,1024,8192]{2,1,0:T(8,128)(2,1)} %param.12), kind=kOutput, calls=%fused_computation.13 | convolution fusion | flops 6445596672 | bytes 23855104 | tf_op jit(solution)/shard_map/dot_general | solution.py:451
  21.8 2.4 constant_dynamic-slice_fusion.5
  24.1 1.7 copy-done.10
  26.4 1.6 collective-permute-done.1
  27.9 1.8 collective-permute-start.3
  29.8 3.7 add_convert_fusion.5
  33.5 8.4 %collective-permute-start.8 = (bf16[384,2048]{1,0:T(8,128)(2,1)}, bf16[384,2048]{1,0:T(8,128)(2,1)}, u32[]{:S(2)}, u32[]{:S(2)}) collective-permute-start(bf16[384,2048]{1,0:T(8,128)(2,1)} %add_convert_fusion.5), channel_id=1, source_target_pairs={{0,2},{7,5},{8,10},{15,13},{16,18},{23,21},{24,26},{31,29}} | collective-permute-start | bytes 4718600 | tf_op jit(solution)/shard_map/ppermute | solution.py:320
  42.7 1.6 turn.2
  45.0 14.0 %collective-permute-done.8 = bf16[384,2048]{1,0:T(8,128)(2,1)} collective-permute-done((bf16[384,2048]{1,0:T(8,128)(2,1)}, bf16[384,2048]{1,0:T(8,128)(2,1)}, u32[]{:S(2)}, u32[]{:S(2)}) %collective-permute-start.8) | collective-permute-done | bytes 1572896 | tf_op jit(solution)/shard_map/ppermute | solution.py:320
  59.0 3.3 add_convert_fusion.4
  62.3 4.5 collective-permute-start.13
  66.8 1.8 select_dynamic-update-slice_fusion.11
  68.6 1.7 select_dynamic-update-slice_fusion.10
  70.3 1.8 select_dynamic-update-slice_fusion.9
  72.1 1.9 collective-permute-start.9
  74.0 10.6 %collective-permute-done.13 = bf16[384,2048]{1,0:T(8,128)(2,1)S(1)} collective-permute-done((bf16[384,2048]{1,0:T(8,128)(2,1)S(1)}, bf16[384,2048]{1,0:T(8,128)(2,1)S(1)}, u32[]{:S(2)}, u32[]{:S(2)}) %collective-permute-start.13) | collective-permute-done | bytes 1572896 | tf_op jit(solution)/shard_map/ppermute | solution.py:320
  84.6 3.5 add_convert_fusion.3
  88.1 5.9 %collective-permute-start.14 = (bf16[384,2048]{1,0:T(8,128)(2,1)}, bf16[384,2048]{1,0:T(8,128)(2,1)}, u32[]{:S(2)}, u32[]{:S(2)}) collective-permute-start(bf16[384,2048]{1,0:T(8,128)(2,1)} %add_convert_fusion.3), channel_id=1, source_target_pairs={{0,2},{2,4},{4,6},{3,1},{5,3},{7,5},{8,10},{10,12},{12,14},{11,9},... | collective-permute-start | bytes 4718600 | tf_op jit(solution)/shard_map/ppermute | solution.py:320
  96.5 13.1 %fusion.21 = (bf16[384,1024]{1,0:T(8,128)(2,1)S(1)}, f32[384,1024]{1,0:T(8,128)}) fusion(bf16[384,1024]{1,0:T(8,128)(2,1)S(1)} %copy-done.13, f32[1024]{0:T(1024)S(1)} %bitcast.44, bf16[384,8192]{1,0:T(8,128)(2,1)S(1)} %select_dynamic-update-slice_fusion.6.refs_3_, bf16[2,1024,8192]{2,1,0:T(8,128)(2,1)} %param.12), kind=kOutput, calls=%fused_computation.31 | convolution fusion | flops 6444417024 | bytes 26218496 | tf_op jit(solution)/shard_map/dot_general | solution.py:445
  110.7 2.8 add_convert_fusion.7
  113.5 4.9 %constant_dynamic-slice_fusion.4 = bf16[384,4096]{1,0:T(8,128)(2,1)} fusion(bf16[384,8192]{1,0:T(8,128)(2,1)} %copy-done.1, s32[]{:T(128)S(6)} %select_n.370), kind=kLoop, calls=%fused_computation.56 | loop fusion | bytes 6291460 | tf_op jit(solution)/shard_map/dynamic_slice | solution.py:416
  118.4 3.9 constant_dynamic-update-slice_fusion
  122.2 5.5 %collective-permute-start.11 = (bf16[384,2048]{1,0:T(8,128)(2,1)}, bf16[384,2048]{1,0:T(8,128)(2,1)}, u32[]{:S(2)}, u32[]{:S(2)}) collective-permute-start(bf16[384,2048]{1,0:T(8,128)(2,1)} %get-tuple-element.89), channel_id=1, source_target_pairs={{0,2},{2,4},{4,6},{3,1},{5,3},{7,5},{8,10},{10,12},{12,14},{11,9},... | collective-permute-start | bytes 4718600 | tf_op jit(solution)/shard_map/ppermute | solution.py:320
  127.8 2.3 convert_add_fusion.1
  131.5 10.3 %fusion.15 = bf16[384,8192]{1,0:T(8,128)(2,1)S(1)} fusion(bf16[384,1024]{1,0:T(8,128)(2,1)S(1)} %fusion.22.value_ref, bf16[2,1024,8192]{2,1,0:T(8,128)(2,1)} %param.12), kind=kOutput, calls=%fused_computation.14 | convolution fusion | flops 6445596672 | bytes 23855104 | tf_op jit(solution)/shard_map/dot_general | solution.py:451
  141.8 2.4 constant_dynamic-slice_fusion
  144.2 1.7 copy-done.11
  147.7 2.0 collective-permute-start.17
  149.7 3.4 add_convert_fusion.2
  153.1 5.1 %collective-permute-start.22 = (bf16[96,8192]{1,0:T(8,128)(2,1)}, bf16[96,8192]{1,0:T(8,128)(2,1)}, u32[]{:S(2)}, u32[]{:S(2)}) collective-permute-start(bf16[96,8192]{1,0:T(8,128)(2,1)} %add_convert_fusion.2), channel_id=1, source_target_pairs={{0,2},{7,5},{8,10},{15,13},{16,18},{23,21},{24,26},{31,29}} | collective-permute-start | bytes 4718600 | tf_op jit(solution)/shard_map/ppermute | solution.py:320
  159.3 24.2 %collective-permute-done.24.refs_4_ = bf16[384,4096]{1,0:T(8,128)(2,1)} collective-permute-done((bf16[384,4096]{1,0:T(8,128)(2,1)}, bf16[384,4096]{1,0:T(8,128)(2,1)}, u32[]{:S(2)}, u32[]{:S(2)}) %collective-permute-start.24) | collective-permute-done | bytes 3145760 | tf_op jit(solution)/shard_map/ppermute | solution.py:388
  183.5 3.4 select_dynamic-update-slice_fusion.5
  188.4 1.5 collective-permute-start.25
  190.7 4.1 add_convert_fusion.1
  195.3 1.8 select_dynamic-update-slice_fusion.4
  198.5 9.3 %half_grad.4 = (bf16[256,4096]{1,0:T(8,128)(2,1)S(1)}, bf16[256,4096]{1,0:T(8,128)(2,1)}) custom-call(s32[3]{0:T(128)S(1)} %pad_add_fusion.1.index_ref, bf16[1024,384]{1,0:T(8,128)(2,1)S(1)} %get-tuple-element.57.refs_0_.refs_1_, bf16[1024,384]{1,0:T(8,128)(2,1)S(1)} %get-tuple-element.57.refs_0_.refs_1_, ...), custom_call_target="tpu_custom_call" | custom-call | flops 3221225472 | bytes 10485760 | tf_op jit(solution)/shard_map/half_grad/pallas_call | solution.py:142
  209.2 4.1 collective-permute-start.29
  213.3 7.6 %half_grad.5 = (bf16[256,4096]{1,0:T(8,128)(2,1)S(1)}, bf16[256,4096]{1,0:T(8,128)(2,1)}) custom-call(s32[3]{0:T(128)S(1)} %pad_add_fusion.2.index_ref, bf16[1024,384]{1,0:T(8,128)(2,1)S(1)} %get-tuple-element.57.refs_0_.refs_1_, bf16[1024,384]{1,0:T(8,128)(2,1)S(1)} %get-tuple-element.57.refs_0_.refs_1_, ...), custom_call_target="tpu_custom_call" | custom-call | flops 3221225472 | bytes 10485760 | tf_op jit(solution)/shard_map/half_grad/pallas_call | solution.py:142
  220.9 4.0 select_dynamic-update-slice_fusion.3
  224.9 1.8 select_dynamic-update-slice_fusion.2
  226.7 3.2 select_dynamic-update-slice_fusion.1
  229.9 1.8 select_dynamic-update-slice_fusion.refs_3_
  232.6 13.0 %fusion.19 = bf16[384,1024]{1,0:T(8,128)(2,1)} fusion(bf16[384,1024]{1,0:T(8,128)(2,1)S(1)} %copy-done.19, f32[384,1024]{1,0:T(8,128)S(1)} %copy-done.15, f32[384,1024]{1,0:T(8,128)S(1)} %copy-done.27, bf16[384,8192]{1,0:T(8,128)(2,1)} %select_dynamic-update-slice_fusion.refs_3_, bf16[2,1024,8192]{2,1,0:T(8,128)(2,1)} %param.12, f32[1024]{0:T(1024)S(1)} %bitcast.43, ...), kind=kOutput, calls=%fused_computation.29 | convolution fusion | flops 6445596672 | bytes 27795456 | tf_op jit(solution)/shard_map/dot_general | solution.py:445
  245.6 4.8 %constant_dynamic-slice_fusion.1 = bf16[384,4096]{1,0:T(8,128)(2,1)} fusion(bf16[384,8192]{1,0:T(8,128)(2,1)} %select_dynamic-update-slice_fusion.refs_3_, s32[]{:T(128)S(6)} %select_n.383), kind=kLoop, calls=%fused_computation.53 | loop fusion | bytes 6291460 | tf_op jit(solution)/shard_map/dynamic_slice | solution.py:416
  251.1 4.1 add_convert_fusion
  255.2 2.7 collective-permute-start.30
  257.9 17.9 %collective-permute-done.30 = bf16[96,8192]{1,0:T(8,128)(2,1)S(1)} collective-permute-done((bf16[96,8192]{1,0:T(8,128)(2,1)}, bf16[96,8192]{1,0:T(8,128)(2,1)S(1)}, u32[]{:S(2)}, u32[]{:S(2)}) %collective-permute-start.30) | collective-permute-done | bytes 1572896 | tf_op jit(solution)/shard_map/ppermute | solution.py:320
  275.8 12.2 %collective-permute-done.33.refs_4_ = bf16[384,4096]{1,0:T(8,128)(2,1)} collective-permute-done((bf16[384,4096]{1,0:T(8,128)(2,1)}, bf16[384,4096]{1,0:T(8,128)(2,1)}, u32[]{:S(2)}, u32[]{:S(2)}) %collective-permute-start.33) | collective-permute-done | bytes 3145760 | tf_op jit(solution)/shard_map/ppermute | solution.py:388
  288.0 2.3 add_convert_fusion.6
  294.6 3.5 all-to-all-start
  300.4 2.0 convert_add_fusion.2.summed_ref
  302.5 16.6 %all-to-all-done.late_ref = bf16[8,48,1024]{2,1,0:T(8,128)(2,1)S(1)} async-done(((bf16[8,48,1024]{2,1,0:T(8,128)(2,1)}), bf16[8,48,1024]{2,1,0:T(8,128)(2,1)S(1)}, u32[]{:S(2)}, u32[]{:S(2)}) %all-to-all-start) | async-done | bytes 786464 | tf_op jit(solution)/shard_map/all_to_all | solution.py:486
  319.1 4.7 %to_slots.1 = bf16[32,2,48,128]{3,2,1,0:T(8,128)(2,1)} custom-call(s32[128]{0:T(128)S(1)} %scatter_custom_fusion.table_ref, f32[48,8192]{1,0:T(8,128)S(1)} %convert_add_fusion.2.summed_ref, bf16[8,48,1024]{2,1,0:T(8,128)(2,1)S(1)} %all-to-all-done.late_ref), custom_call_target="tpu_custom_call" | custom-call | flops 1572864 | bytes 3932160 | tf_op jit(solution)/shard_map/to_slots/pallas_call | solution.py:265
  323.8 10.0 %half_grad.6 = (bf16[256,4096]{1,0:T(8,128)(2,1)S(1)}, bf16[256,4096]{1,0:T(8,128)(2,1)}) custom-call(s32[3]{0:T(128)S(1)} %pad_add_fusion.1.index_ref, bf16[1024,384]{1,0:T(8,128)(2,1)S(1)} %get-tuple-element.49.refs_0_.refs_1_, bf16[1024,384]{1,0:T(8,128)(2,1)S(1)} %get-tuple-element.49.refs_0_.refs_1_, ...), custom_call_target="tpu_custom_call" | custom-call | flops 3221225472 | bytes 10485760 | tf_op jit(solution)/shard_map/half_grad/pallas_call | solution.py:142
  336.7 10.0 %half_grad.7 = (bf16[256,4096]{1,0:T(8,128)(2,1)S(1)}, bf16[256,4096]{1,0:T(8,128)(2,1)}) custom-call(s32[3]{0:T(128)S(1)} %pad_add_fusion.2.index_ref, bf16[1024,384]{1,0:T(8,128)(2,1)S(1)} %get-tuple-element.49.refs_0_.refs_1_, bf16[1024,384]{1,0:T(8,128)(2,1)S(1)} %get-tuple-element.49.refs_0_.refs_1_, ...), custom_call_target="tpu_custom_call" | custom-call | flops 3221225472 | bytes 10485760 | tf_op jit(solution)/shard_map/half_grad/pallas_call | solution.py:142
  348.6 2.8 all-to-all-start.1
  352.4 1.6 copy-done.5
  354.0 8.5 %weight_update.2 = (f32[2,256,8192]{2,1,0:T(8,128)}, f32[256,1]{1,0:T(8,128)S(1)}) custom-call(s32[1]{0:T(128)} %bitcast.side_ref, f32[256,1]{1,0:T(8,128)S(1)} %copy.15.accum_ref, bf16[256,4096]{1,0:T(8,128)(2,1)S(1)} %copy-done.3, bf16[256,4096]{1,0:T(8,128)(2,1)} %collective-permute-done.36.refs_1_, bf16[256,4096]{1,0:T(8,128)(2,1)S(1)} %copy-done.5, ...), custom_call_target="tpu_custom_call" | custom-call | flops 8388608 | bytes 16777216 | tf_op jit(solution)/shard_map/weight_update/pallas_call | solution.py:208
  362.6 39.8 %all-to-all-done.1.g_ref = bf16[32,2,48,128]{3,2,1,0:T(8,128)(2,1)S(1)} async-done(((bf16[32,2,48,128]{3,2,1,0:T(8,128)(2,1)}), bf16[32,2,48,128]{3,2,1,0:T(8,128)(2,1)S(1)}, u32[]{:S(2)}, u32[]{:S(2)}) %all-to-all-start.1) | async-done | bytes 786464 | tf_op jit(solution)/shard_map/all_to_all | solution.py:501
  403.3 48.0 %embed_update.1 = (f32[4,64,8192]{2,1,0:T(8,128)}, f32[4,8192]{1,0:T(4,128)}) custom-call(s32[24576]{0:T(1024)} %reshape.15.ids_ref, bf16[32,2,48,128]{3,2,1,0:T(8,128)(2,1)} %copy-done.16, f32[4,64,8192]{2,1,0:T(8,128)} %bitcast.40, f32[4,8192]{1,0:T(4,128)} %acc_in_ref.1), custom_call_target="tpu_custom_call" | custom-call | flops 100000000 | bytes 150000000 | tf_op jit(solution)/shard_map/embed_update/pallas_call | solution.py:57
  451.3 8.5 %weight_update.3 = (f32[2,256,8192]{2,1,0:T(8,128)}, f32[256,1]{1,0:T(8,128)S(1)}) custom-call(s32[1]{0:T(128)} %bitcast.side_ref, f32[256,1]{1,0:T(8,128)S(1)} %copy.16.accum_ref, bf16[256,4096]{1,0:T(8,128)(2,1)S(1)} %copy-done.7, bf16[256,4096]{1,0:T(8,128)(2,1)} %collective-permute-done.38.refs_1_, ...), custom_call_target="tpu_custom_call", output_to_operand_aliasing={{0}: (6, {})} | custom-call | flops 8388608 | bytes 16777216 | tf_op jit(solution)/shard_map/weight_update/pallas_call | solution.py:208
  (146 shorter events, 31.8 us)
Async XLA Ops:
  0.6 2.7 collective-permute-start
  1.2 2.1 copy-start.12
  1.2 10.0 %copy-start.17 = (bf16[384,1024]{1,0:T(8,128)(2,1)S(1)}, bf16[384,1024]{1,0:T(8,128)(2,1)}, u32[]{:S(2)}) copy-start(bf16[384,1024]{1,0:T(8,128)(2,1)} %param.11) | copy-start | bytes 2359300
  5.2 22.8 %collective-permute-start.1 = (bf16[384,2048]{1,0:T(8,128)(2,1)S(1)}, bf16[384,2048]{1,0:T(8,128)(2,1)}, u32[]{:S(2)}, u32[]{:S(2)}) collective-permute-start(bf16[384,2048]{1,0:T(8,128)(2,1)S(1)} %get-tuple-element.91), channel_id=1, source_target_pairs={{0,2},{2,4},{4,6},{3,1},{5,3},{7,5},{8,10},{10,12},{12,14},{11,9},... | collective-permute-start | bytes 4718600 | tf_op jit(solution)/shard_map/ppermute | solution.py:320
  21.7 4.1 copy-start.10
  25.9 3.9 collective-permute-start.4
  25.9 16.2 %copy-start.24 = (f32[2,1024]{1,0:T(2,128)S(1)}, f32[2,1024]{1,0:T(2,128)}, u32[]{:S(2)}) copy-start(f32[2,1024]{1,0:T(2,128)} %param.13) | copy-start | bytes 24580
  25.9 19.2 %collective-permute-start.7 = (bf16[384,2048]{1,0:T(8,128)(2,1)}, bf16[384,2048]{1,0:T(8,128)(2,1)}, u32[]{:S(2)}, u32[]{:S(2)}) collective-permute-start(bf16[384,2048]{1,0:T(8,128)(2,1)} %get-tuple-element.96), channel_id=1, source_target_pairs={{0,1},{1,0},{2,3},{3,2},{4,5},{5,4},{6,7},{7,6},{8,9},{9,8},{10,11... | collective-permute-start | bytes 4718600 | tf_op jit(solution)/shard_map/ppermute | solution.py:315
  27.9 16.3 %collective-permute-start.3 = (bf16[384,2048]{1,0:T(8,128)(2,1)}, bf16[384,2048]{1,0:T(8,128)(2,1)}, u32[]{:S(2)}, u32[]{:S(2)}) collective-permute-start(bf16[384,2048]{1,0:T(8,128)(2,1)} %collective-permute-done.1), channel_id=1, source_target_pairs={{2,4},{4,6},{3,1},{5,3},{10,12},{12,14},{11,9},{13,11},{18,20},{20... | collective-permute-start | bytes 4718600 | tf_op jit(solution)/shard_map/ppermute | solution.py:320
  33.5 25.5 %collective-permute-start.8 = (bf16[384,2048]{1,0:T(8,128)(2,1)}, bf16[384,2048]{1,0:T(8,128)(2,1)}, u32[]{:S(2)}, u32[]{:S(2)}) collective-permute-start(bf16[384,2048]{1,0:T(8,128)(2,1)} %add_convert_fusion.5), channel_id=1, source_target_pairs={{0,2},{7,5},{8,10},{15,13},{16,18},{23,21},{24,26},{31,29}} | collective-permute-start | bytes 4718600 | tf_op jit(solution)/shard_map/ppermute | solution.py:320
  41.9 26.7 %collective-permute-start.2 = (bf16[384,2048]{1,0:T(8,128)(2,1)}, bf16[384,2048]{1,0:T(8,128)(2,1)S(1)}, u32[]{:S(2)}, u32[]{:S(2)}) collective-permute-start(bf16[384,2048]{1,0:T(8,128)(2,1)} %collective-permute-done.1), channel_id=1, source_target_pairs={{0,1},{1,0},{2,3},{3,2},{4,5},{5,4},{6,7},{7,6},{8,9},{9,8},{10,11... | collective-permute-start | bytes 4718600 | tf_op jit(solution)/shard_map/ppermute | solution.py:315
  42.1 31.9 %collective-permute-start.12 = (bf16[384,2048]{1,0:T(8,128)(2,1)}, bf16[384,2048]{1,0:T(8,128)(2,1)S(1)}, u32[]{:S(2)}, u32[]{:S(2)}) collective-permute-start(bf16[384,2048]{1,0:T(8,128)(2,1)} %get-tuple-element.95), channel_id=1, source_target_pairs={{0,1},{1,0},{2,3},{3,2},{4,5},{5,4},{6,7},{7,6},{8,9},{9,8},{10,11... | collective-permute-start | bytes 4718600 | tf_op jit(solution)/shard_map/ppermute | solution.py:315
  44.3 27.8 %collective-permute-start.6 = (bf16[384,2048]{1,0:T(8,128)(2,1)}, bf16[384,2048]{1,0:T(8,128)(2,1)S(1)}, u32[]{:S(2)}, u32[]{:S(2)}) collective-permute-start(bf16[384,2048]{1,0:T(8,128)(2,1)} %collective-permute-done.3), channel_id=1, source_target_pairs={{4,6},{3,1},{12,14},{11,9},{20,22},{19,17},{28,30},{27,25}} | collective-permute-start | bytes 4718600 | tf_op jit(solution)/shard_map/ppermute | solution.py:320
  62.3 22.3 %collective-permute-start.13 = (bf16[384,2048]{1,0:T(8,128)(2,1)S(1)}, bf16[384,2048]{1,0:T(8,128)(2,1)S(1)}, u32[]{:S(2)}, u32[]{:S(2)}) collective-permute-start(bf16[384,2048]{1,0:T(8,128)(2,1)S(1)} %add_convert_fusion.4), channel_id=1, source_target_pairs={{0,2},{2,4},{5,3},{7,5},{8,10},{10,12},{13,11},{15,13},{16,18},{18... | collective-permute-start | bytes 4718600 | tf_op jit(solution)/shard_map/ppermute | solution.py:320
  68.6 25.5 %collective-permute-start.5 = (bf16[384,2048]{1,0:T(8,128)(2,1)}, bf16[384,2048]{1,0:T(8,128)(2,1)S(1)}, u32[]{:S(2)}, u32[]{:S(2)}) collective-permute-start(bf16[384,2048]{1,0:T(8,128)(2,1)} %collective-permute-done.3), channel_id=1, source_target_pairs={{0,1},{1,0},{2,3},{3,2},{4,5},{5,4},{6,7},{7,6},{8,9},{9,8},{10,11... | collective-permute-start | bytes 4718600 | tf_op jit(solution)/shard_map/ppermute | solution.py:315
  72.1 22.0 %copy-start = (bf16[384,8192]{1,0:T(8,128)(2,1)S(1)}, bf16[384,8192]{1,0:T(8,128)(2,1)}, u32[]{:S(2)}) copy-start(bf16[384,8192]{1,0:T(8,128)(2,1)} %select_dynamic-update-slice_fusion.9) | copy-start | bytes 18874372
  72.1 23.3 %collective-permute-start.9 = (bf16[384,2048]{1,0:T(8,128)(2,1)S(1)}, bf16[384,2048]{1,0:T(8,128)(2,1)S(1)}, u32[]{:S(2)}, u32[]{:S(2)}) collective-permute-start(bf16[384,2048]{1,0:T(8,128)(2,1)S(1)} %collective-permute-done.6), channel_id=1, source_target_pairs={{0,1},{1,0},{2,3},{3,2},{4,5},{5,4},{6,7},{7,6},{8,9},{9,8},{10,11... | collective-permute-start | bytes 4718600 | tf_op jit(solution)/shard_map/ppermute | solution.py:315
  88.1 22.6 %collective-permute-start.14 = (bf16[384,2048]{1,0:T(8,128)(2,1)}, bf16[384,2048]{1,0:T(8,128)(2,1)}, u32[]{:S(2)}, u32[]{:S(2)}) collective-permute-start(bf16[384,2048]{1,0:T(8,128)(2,1)} %add_convert_fusion.3), channel_id=1, source_target_pairs={{0,2},{2,4},{4,6},{3,1},{5,3},{7,5},{8,10},{10,12},{12,14},{11,9},... | collective-permute-start | bytes 4718600 | tf_op jit(solution)/shard_map/ppermute | solution.py:320
  96.1 13.5 %copy-start.1 = (bf16[384,8192]{1,0:T(8,128)(2,1)}, bf16[384,8192]{1,0:T(8,128)(2,1)S(1)}, u32[]{:S(2)}) copy-start(bf16[384,8192]{1,0:T(8,128)(2,1)S(1)} %select_dynamic-update-slice_fusion.6.refs_3_) | copy-start | bytes 18874372
  109.6 8.8 %collective-permute-start.10 = (bf16[384,1024]{1,0:T(8,128)(2,1)S(1)}, bf16[384,1024]{1,0:T(8,128)(2,1)}, u32[]{:S(2)}, u32[]{:S(2)}) collective-permute-start(bf16[384,1024]{1,0:T(8,128)(2,1)S(1)} %get-tuple-element.102), channel_id=1, source_target_pairs={{0,1},{1,0},{2,3},{3,2},{4,5},{5,4},{6,7},{7,6},{8,9},{9,8},{10,11... | collective-permute-start | bytes 2359304 | tf_op jit(solution)/shard_map/ppermute | solution.py:315
  113.5 14.3 %collective-permute-start.15 = (bf16[384,1024]{1,0:T(8,128)(2,1)}, bf16[384,1024]{1,0:T(8,128)(2,1)}, u32[]{:S(2)}, u32[]{:S(2)}) collective-permute-start(bf16[384,1024]{1,0:T(8,128)(2,1)} %add_convert_fusion.7), channel_id=1, source_target_pairs={{0,1},{1,0},{2,3},{3,2},{4,5},{5,4},{6,7},{7,6},{8,9},{9,8},{10,11... | collective-permute-start | bytes 2359304 | tf_op jit(solution)/shard_map/ppermute | solution.py:315
  118.4 9.4 %copy-start.18 = (bf16[384,1024]{1,0:T(8,128)(2,1)S(1)}, bf16[384,1024]{1,0:T(8,128)(2,1)}, u32[]{:S(2)}) copy-start(bf16[384,1024]{1,0:T(8,128)(2,1)} %param.11) | copy-start | bytes 2359300
  122.2 25.4 %collective-permute-start.11 = (bf16[384,2048]{1,0:T(8,128)(2,1)}, bf16[384,2048]{1,0:T(8,128)(2,1)}, u32[]{:S(2)}, u32[]{:S(2)}) collective-permute-start(bf16[384,2048]{1,0:T(8,128)(2,1)} %get-tuple-element.89), channel_id=1, source_target_pairs={{0,2},{2,4},{4,6},{3,1},{5,3},{7,5},{8,10},{10,12},{12,14},{11,9},... | collective-permute-start | bytes 4718600 | tf_op jit(solution)/shard_map/ppermute | solution.py:320
  141.8 4.1 copy-start.11
  145.9 3.8 collective-permute-start.18
  145.9 37.6 %collective-permute-start.24 = (bf16[384,4096]{1,0:T(8,128)(2,1)}, bf16[384,4096]{1,0:T(8,128)(2,1)}, u32[]{:S(2)}, u32[]{:S(2)}) collective-permute-start(bf16[384,4096]{1,0:T(8,128)(2,1)} %constant_dynamic-slice_fusion.4), channel_id=1, source_target_pairs={{0,8},{1,17},{2,10},{3,19},{4,12},{5,21},{6,14},{7,23},{8,0},{9,25... | collective-permute-start | bytes 9437192 | tf_op jit(solution)/shard_map/ppermute | solution.py:388
  147.4 41.0 %collective-permute-start.21 = (bf16[96,8192]{1,0:T(8,128)(2,1)}, bf16[96,8192]{1,0:T(8,128)(2,1)}, u32[]{:S(2)}, u32[]{:S(2)}) collective-permute-start(bf16[96,8192]{1,0:T(8,128)(2,1)} %get-tuple-element.93), channel_id=1, source_target_pairs={{0,1},{1,0},{2,3},{3,2},{4,5},{5,4},{6,7},{7,6},{8,9},{9,8},{10,11... | collective-permute-start | bytes 4718600 | tf_op jit(solution)/shard_map/ppermute | solution.py:315
  147.7 39.2 %collective-permute-start.17 = (bf16[384,2048]{1,0:T(8,128)(2,1)}, bf16[384,2048]{1,0:T(8,128)(2,1)}, u32[]{:S(2)}, u32[]{:S(2)}) collective-permute-start(bf16[384,2048]{1,0:T(8,128)(2,1)} %collective-permute-done.11), channel_id=1, source_target_pairs={{2,4},{4,6},{3,1},{5,3},{10,12},{12,14},{11,9},{13,11},{18,20},{20... | collective-permute-start | bytes 4718600 | tf_op jit(solution)/shard_map/ppermute | solution.py:320
  153.1 36.8 %collective-permute-start.22 = (bf16[96,8192]{1,0:T(8,128)(2,1)}, bf16[96,8192]{1,0:T(8,128)(2,1)}, u32[]{:S(2)}, u32[]{:S(2)}) collective-permute-start(bf16[96,8192]{1,0:T(8,128)(2,1)} %add_convert_fusion.2), channel_id=1, source_target_pairs={{0,2},{7,5},{8,10},{15,13},{16,18},{23,21},{24,26},{31,29}} | collective-permute-start | bytes 4718600 | tf_op jit(solution)/shard_map/ppermute | solution.py:320
  158.4 36.4 %collective-permute-start.16 = (bf16[384,2048]{1,0:T(8,128)(2,1)}, bf16[384,2048]{1,0:T(8,128)(2,1)S(1)}, u32[]{:S(2)}, u32[]{:S(2)}) collective-permute-start(bf16[384,2048]{1,0:T(8,128)(2,1)} %collective-permute-done.11), channel_id=1, source_target_pairs={{0,1},{1,0},{2,3},{3,2},{4,5},{5,4},{6,7},{7,6},{8,9},{9,8},{10,11... | collective-permute-start | bytes 4718600 | tf_op jit(solution)/shard_map/ppermute | solution.py:315
  183.5 29.8 %collective-permute-start.26 = (bf16[384,4096]{1,0:T(8,128)(2,1)}, bf16[384,4096]{1,0:T(8,128)(2,1)S(1)}, u32[]{:S(2)}, u32[]{:S(2)}) collective-permute-start(bf16[384,4096]{1,0:T(8,128)(2,1)} %collective-permute-done.24.refs_4_), channel_id=1, source_target_pairs={{0,1},{1,0},{2,3},{3,2},{4,5},{5,4},{6,7},{7,6},{8,9},{9,8},{10,11... | collective-permute-start | bytes 9437192 | tf_op jit(solution)/shard_map/ppermute | solution.py:315
  183.5 15.0 %slice-start = ((s8[6291456]{0:T(1024)(128)(4,1)}), s8[4194304]{0:T(1024)(128)(4,1)S(1)}, s32[]{:S(2)}) async-start(s8[6291456]{0:T(1024)(128)(4,1)} %bitcast.38), calls=%async_computation.2 | async-start | bytes 8388608
  186.9 11.2 %collective-permute-start.23 = (bf16[2,256,384]{2,1,0:T(8,128)(2,1)S(1)}, bf16[2,256,384]{2,1,0:T(8,128)(2,1)S(1)}, u32[]{:S(2)}, u32[]{:S(2)}) collective-permute-start(bf16[2,256,384]{2,1,0:T(8,128)(2,1)S(1)} %get-tuple-element.60), channel_id=1, source_target_pairs={{0,8},{1,17},{2,10},{3,19},{4,12},{5,21},{6,14},{7,23},{8,0},{9,25... | collective-permute-start | bytes 1179656 | tf_op jit(solution)/shard_map/ppermute | solution.py:388
  188.4 10.1 %slice-start.1 = ((s8[6291456]{0:T(1024)(128)(4,1)}), s8[2097152]{0:T(1024)(128)(4,1)S(1)}, s32[]{:S(2)}) async-start(s8[6291456]{0:T(1024)(128)(4,1)} %bitcast.38), calls=%async_computation.3 | async-start | bytes 4194304
  188.4 20.8 %collective-permute-start.25 = (bf16[2,256,384]{2,1,0:T(8,128)(2,1)S(1)}, bf16[2,256,384]{2,1,0:T(8,128)(2,1)S(1)}, u32[]{:S(2)}, u32[]{:S(2)}) collective-permute-start(bf16[2,256,384]{2,1,0:T(8,128)(2,1)S(1)} %get-tuple-element.63), channel_id=1, source_target_pairs={{0,16},{1,9},{2,18},{3,11},{4,20},{5,13},{6,22},{7,15},{8,24},{9,1... | collective-permute-start | bytes 1179656 | tf_op jit(solution)/shard_map/ppermute | solution.py:388
  189.9 31.0 %collective-permute-start.20 = (bf16[384,2048]{1,0:T(8,128)(2,1)}, bf16[384,2048]{1,0:T(8,128)(2,1)S(1)}, u32[]{:S(2)}, u32[]{:S(2)}) collective-permute-start(bf16[384,2048]{1,0:T(8,128)(2,1)} %collective-permute-done.17), channel_id=1, source_target_pairs={{4,6},{3,1},{12,14},{11,9},{20,22},{19,17},{28,30},{27,25}} | collective-permute-start | bytes 4718600 | tf_op jit(solution)/shard_map/ppermute | solution.py:320
  194.8 30.1 %collective-permute-start.19 = (bf16[384,2048]{1,0:T(8,128)(2,1)}, bf16[384,2048]{1,0:T(8,128)(2,1)S(1)}, u32[]{:S(2)}, u32[]{:S(2)}) collective-permute-start(bf16[384,2048]{1,0:T(8,128)(2,1)} %collective-permute-done.17), channel_id=1, source_target_pairs={{0,1},{1,0},{2,3},{3,2},{4,5},{5,4},{6,7},{7,6},{8,9},{9,8},{10,11... | collective-permute-start | bytes 4718600 | tf_op jit(solution)/shard_map/ppermute | solution.py:315
  198.1 53.0 %collective-permute-start.28 = (bf16[96,8192]{1,0:T(8,128)(2,1)}, bf16[96,8192]{1,0:T(8,128)(2,1)}, u32[]{:S(2)}, u32[]{:S(2)}) collective-permute-start(bf16[96,8192]{1,0:T(8,128)(2,1)} %get-tuple-element.92), channel_id=1, source_target_pairs={{0,1},{1,0},{2,3},{3,2},{4,5},{5,4},{6,7},{7,6},{8,9},{9,8},{10,11... | collective-permute-start | bytes 4718600 | tf_op jit(solution)/shard_map/ppermute | solution.py:315
  209.2 41.9 %collective-permute-start.29 = (bf16[96,8192]{1,0:T(8,128)(2,1)}, bf16[96,8192]{1,0:T(8,128)(2,1)}, u32[]{:S(2)}, u32[]{:S(2)}) collective-permute-start(bf16[96,8192]{1,0:T(8,128)(2,1)} %add_convert_fusion.1), channel_id=1, source_target_pairs={{0,2},{2,4},{5,3},{7,5},{8,10},{10,12},{13,11},{15,13},{16,18},{18... | collective-permute-start | bytes 4718600 | tf_op jit(solution)/shard_map/ppermute | solution.py:320
  220.9 4.0 copy-start.4
  220.9 9.0 %collective-permute-start.27 = (bf16[384,2048]{1,0:T(8,128)(2,1)S(1)}, bf16[384,2048]{1,0:T(8,128)(2,1)S(1)}, u32[]{:S(2)}, u32[]{:S(2)}) collective-permute-start(bf16[384,2048]{1,0:T(8,128)(2,1)S(1)} %collective-permute-done.20), channel_id=1, source_target_pairs={{0,1},{1,0},{2,3},{3,2},{4,5},{5,4},{6,7},{7,6},{8,9},{9,8},{10,11... | collective-permute-start | bytes 4718600 | tf_op jit(solution)/shard_map/ppermute | solution.py:315
  229.9 1.8 copy-start.15
  229.9 1.8 copy-start.19
  229.9 2.7 copy-start.27
  250.4 37.6 %collective-permute-start.33 = (bf16[384,4096]{1,0:T(8,128)(2,1)}, bf16[384,4096]{1,0:T(8,128)(2,1)}, u32[]{:S(2)}, u32[]{:S(2)}) collective-permute-start(bf16[384,4096]{1,0:T(8,128)(2,1)} %constant_dynamic-slice_fusion.1), channel_id=1, source_target_pairs={{0,8},{1,17},{2,10},{3,19},{4,12},{5,21},{6,14},{7,23},{8,0},{9,25... | collective-permute-start | bytes 9437192 | tf_op jit(solution)/shard_map/ppermute | solution.py:388
  255.2 35.7 %copy-start.26 = (s32[128]{0:T(128)S(1)}, s32[128]{0:T(128)}, u32[]{:S(2)}) copy-start(s32[128]{0:T(128)} %param.15) | copy-start | bytes 1540
  255.2 20.7 %collective-permute-start.30 = (bf16[96,8192]{1,0:T(8,128)(2,1)}, bf16[96,8192]{1,0:T(8,128)(2,1)S(1)}, u32[]{:S(2)}, u32[]{:S(2)}) collective-permute-start(bf16[96,8192]{1,0:T(8,128)(2,1)} %add_convert_fusion), channel_id=1, source_target_pairs={{0,2},{2,4},{4,6},{3,1},{5,3},{7,5},{8,10},{10,12},{12,14},{11,9},... | collective-permute-start | bytes 4718600 | tf_op jit(solution)/shard_map/ppermute | solution.py:320
  275.8 15.0 %copy-start.20 = (bf16[96,8192]{1,0:T(8,128)(2,1)}, bf16[96,8192]{1,0:T(8,128)(2,1)S(1)}, u32[]{:S(2)}) copy-start(bf16[96,8192]{1,0:T(8,128)(2,1)S(1)} %collective-permute-done.30) | copy-start | bytes 4718596
  288.0 48.6 %collective-permute-start.35 = (bf16[384,4096]{1,0:T(8,128)(2,1)}, bf16[384,4096]{1,0:T(8,128)(2,1)}, u32[]{:S(2)}, u32[]{:S(2)}) collective-permute-start(bf16[384,4096]{1,0:T(8,128)(2,1)} %collective-permute-done.33.refs_4_), channel_id=1, source_target_pairs={{0,1},{1,0},{2,3},{3,2},{4,5},{5,4},{6,7},{7,6},{8,9},{9,8},{10,11... | collective-permute-start | bytes 9437192 | tf_op jit(solution)/shard_map/ppermute | solution.py:315
  290.4 7.8 %collective-permute-start.31 = (bf16[48,8192]{1,0:T(8,128)(2,1)}, bf16[48,8192]{1,0:T(8,128)(2,1)S(1)}, u32[]{:S(2)}, u32[]{:S(2)}) collective-permute-start(bf16[48,8192]{1,0:T(8,128)(2,1)} %add_convert_fusion.6), channel_id=1, source_target_pairs={{0,1},{1,0},{2,3},{3,2},{4,5},{5,4},{6,7},{7,6},{8,9},{9,8},{10,11... | collective-permute-start | bytes 2359304 | tf_op jit(solution)/shard_map/ppermute | solution.py:315
  291.9 31.9 %collective-permute-start.32 = (bf16[2,256,384]{2,1,0:T(8,128)(2,1)}, bf16[2,256,384]{2,1,0:T(8,128)(2,1)}, u32[]{:S(2)}, u32[]{:S(2)}) collective-permute-start(bf16[2,256,384]{2,1,0:T(8,128)(2,1)} %get-tuple-element.70), channel_id=1, source_target_pairs={{0,8},{1,17},{2,10},{3,19},{4,12},{5,21},{6,14},{7,23},{8,0},{9,25... | collective-permute-start | bytes 1179656 | tf_op jit(solution)/shard_map/ppermute | solution.py:388
  292.6 44.0 %collective-permute-start.34 = (bf16[2,256,384]{2,1,0:T(8,128)(2,1)S(1)}, bf16[2,256,384]{2,1,0:T(8,128)(2,1)}, u32[]{:S(2)}, u32[]{:S(2)}) collective-permute-start(bf16[2,256,384]{2,1,0:T(8,128)(2,1)S(1)} %get-tuple-element.73), channel_id=1, source_target_pairs={{0,16},{1,9},{2,18},{3,11},{4,20},{5,13},{6,22},{7,15},{8,24},{9,1... | collective-permute-start | bytes 1179656 | tf_op jit(solution)/shard_map/ppermute | solution.py:388
  293.5 58.9 %collective-permute-start.36 = (bf16[256,4096]{1,0:T(8,128)(2,1)}, bf16[256,4096]{1,0:T(8,128)(2,1)}, u32[]{:S(2)}, u32[]{:S(2)}) collective-permute-start(bf16[256,4096]{1,0:T(8,128)(2,1)} %get-tuple-element.76), channel_id=1, source_target_pairs={{0,16},{1,9},{2,18},{3,11},{4,20},{5,13},{6,22},{7,15},{8,24},{9,1... | collective-permute-start | bytes 6291464 | tf_op jit(solution)/shard_map/ppermute | solution.py:388
  294.6 24.4 %all-to-all-start = ((bf16[8,48,1024]{2,1,0:T(8,128)(2,1)}), bf16[8,48,1024]{2,1,0:T(8,128)(2,1)S(1)}, u32[]{:S(2)}, u32[]{:S(2)}) async-start(bf16[8,48,1024]{2,1,0:T(8,128)(2,1)} %bitcast.7), calls=%async_computation | async-start | bytes 1572864 | tf_op jit(solution)/shard_map/all_to_all | solution.py:486
  299.1 53.3 %collective-permute-start.37 = (bf16[256,4096]{1,0:T(8,128)(2,1)}, bf16[256,4096]{1,0:T(8,128)(2,1)}, u32[]{:S(2)}, u32[]{:S(2)}) collective-permute-start(bf16[256,4096]{1,0:T(8,128)(2,1)} %get-tuple-element.77), channel_id=1, source_target_pairs={{0,8},{1,17},{2,10},{3,19},{4,12},{5,21},{6,14},{7,23},{8,0},{9,25... | collective-permute-start | bytes 6291464 | tf_op jit(solution)/shard_map/ppermute | solution.py:388
  335.2 116.1 %collective-permute-start.38 = (bf16[256,4096]{1,0:T(8,128)(2,1)}, bf16[256,4096]{1,0:T(8,128)(2,1)}, u32[]{:S(2)}, u32[]{:S(2)}) collective-permute-start(bf16[256,4096]{1,0:T(8,128)(2,1)} %get-tuple-element.82), channel_id=1, source_target_pairs={{0,16},{1,9},{2,18},{3,11},{4,20},{5,13},{6,22},{7,15},{8,24},{9,1... | collective-permute-start | bytes 6291464 | tf_op jit(solution)/shard_map/ppermute | solution.py:388
  336.6 14.7 %copy-start.22 = (s32[4,1536,4]{1,2,0:T(4,128)S(1)}, s32[4,1536,4]{1,2,0:T(4,128)}, u32[]{:S(2)}) copy-start(s32[4,1536,4]{1,2,0:T(4,128)} %param.16) | copy-start | bytes 294916
  336.6 14.7 %copy-start.23 = (s32[4,1536]{1,0:T(4,128)S(1)}, s32[4,1536]{1,0:T(4,128)}, u32[]{:S(2)}) copy-start(s32[4,1536]{1,0:T(4,128)} %param.17) | copy-start | bytes 73732
  336.7 15.4 %copy-start.25 = (f32[2,256]{1,0:T(2,128)S(1)}, f32[2,256]{1,0:T(2,128)}, u32[]{:S(2)}) copy-start(f32[2,256]{1,0:T(2,128)} %param.14) | copy-start | bytes 6148
  348.0 4.4 copy-start.3
  348.0 103.3 %collective-permute-start.39 = (bf16[256,4096]{1,0:T(8,128)(2,1)}, bf16[256,4096]{1,0:T(8,128)(2,1)}, u32[]{:S(2)}, u32[]{:S(2)}) collective-permute-start(bf16[256,4096]{1,0:T(8,128)(2,1)} %get-tuple-element.83), channel_id=1, source_target_pairs={{0,8},{1,17},{2,10},{3,19},{4,12},{5,21},{6,14},{7,23},{8,0},{9,25... | collective-permute-start | bytes 6291464 | tf_op jit(solution)/shard_map/ppermute | solution.py:388
  348.6 53.8 %all-to-all-start.1 = ((bf16[32,2,48,128]{3,2,1,0:T(8,128)(2,1)}), bf16[32,2,48,128]{3,2,1,0:T(8,128)(2,1)S(1)}, u32[]{:S(2)}, u32[]{:S(2)}) async-start(bf16[32,2,48,128]{3,2,1,0:T(8,128)(2,1)} %to_slots.1), calls=%async_computation.1 | async-start | bytes 1572864 | tf_op jit(solution)/shard_map/all_to_all | solution.py:501
  403.3 48.0 %copy-start.7 = (bf16[256,4096]{1,0:T(8,128)(2,1)S(1)}, bf16[256,4096]{1,0:T(8,128)(2,1)}, u32[]{:S(2)}) copy-start(bf16[256,4096]{1,0:T(8,128)(2,1)} %copy-done.6) | copy-start | bytes 6291460
  403.3 48.0 %copy-start.9 = (bf16[256,4096]{1,0:T(8,128)(2,1)S(1)}, bf16[256,4096]{1,0:T(8,128)(2,1)}, u32[]{:S(2)}) copy-start(bf16[256,4096]{1,0:T(8,128)(2,1)} %copy-done.8) | copy-start | bytes 6291460
  (8 other events, 9.8 us)
